TPU v7x, 256 devices: a whole 4x4x8 slice. The times are simulated.
256 devices in a mesh: gx: 32 (over x_hi, z, core), gy: 8 (over x_lo, y).
Axes of the slice: x: 4 (x_hi: 2, x_lo: 2; x = x_hi * 2 + x_lo), y: 4, z: 8, core: 2. Of those that a mesh axis runs over, the one named last changes fastest.
Arguments:
- background: bfloat16 [2, 2048, 1024, 128], P(None, 'gx', 'gy'), may hold values from -6 to 6
- observation_cell_index: int32 [32, 8, 512], P('gx', 'gy'), may hold values from 0 to 16383
- obs_value: float32 [32, 8, 512], P('gx', 'gy'), may hold values from -6 to 6
- obs_inverse: float32 [32, 8, 512], P('gx', 'gy'), may hold values from 0.5 to 4
- obs_count: int32 [32, 8], P('gx', 'gy'), may hold values from 256 to 512, as said below
- taper: int32 [64], replicated, may hold values from 32 to 1024
Outputs:
- analysis: bfloat16 [2, 2048, 1024, 128], P(None, 'gx', 'gy')
Inputs may be any that keep to these rules, and one draw needn't show every extreme that they name: `obs_count`: some tile has exactly 512 live slots and some tile exactly 256.
All inputs are finite; a program needn't handle non-finite values.
Results may differ from a plain program's by a relative error of at most 0.0028.
The roundings to bfloat16 on the way count: a program that leaves them out, or rounds other values in their place, can miss the bound.
Values may be sent and summed in bfloat16 or wider, within the bound.
A program may use at most 64 MiB of HBM per device.

v0:
```python
import jax
import jax.numpy as jnp
from jax import lax
from jax.sharding import PartitionSpec as P

NSTEPS = 6
HIGH = lax.Precision.HIGHEST


def extended(cells, sides, width):
    for axis, dim in sides:
        count = lax.axis_size(axis)
        ends = count - 1
        head = lax.slice_in_dim(cells, 0, width, axis=dim)
        tail = lax.slice_in_dim(cells, cells.shape[dim] - width, cells.shape[dim], axis=dim)
        cells = jnp.concatenate(
            [
                lax.ppermute(tail, axis, [(i, (i + 1) % count) for i in range(ends)]),
                cells,
                lax.ppermute(head, axis, [((i + 1) % count, i) for i in range(ends)]),
            ],
            axis=dim,
        )
    return cells


def observe(ensemble, cell_ids, values, inverse, live_count, tile_x, tile_y):
    picked = jnp.take(ensemble, cell_ids, axis=0).astype(jnp.float32)
    center = jnp.mean(picked, axis=1)
    perturb = (picked - center[:, None]).astype(jnp.bfloat16)
    slot_ids = jnp.arange(cell_ids.shape[0], dtype=jnp.int32)
    live_mask = (slot_ids < live_count).astype(jnp.float32)
    column_pos = cell_ids % (tile_x * tile_y) // tile_y
    row_pos = cell_ids % tile_y
    metadata = jnp.stack(
        [
            values - center,
            inverse * live_mask,
            column_pos.astype(jnp.float32),
            row_pos.astype(jnp.float32),
        ]
    ).astype(jnp.bfloat16)
    return (perturb, metadata, live_mask)


def statistics(perturb, metadata, live_mask):
    members = perturb.shape[1]
    weight = metadata[1].astype(jnp.float32)
    innovation = metadata[0].astype(jnp.float32)
    spread = jnp.sum(jnp.square(perturb.astype(jnp.float32)), axis=1) / (members - 1)
    return (
        jnp.sum(weight * innovation * innovation),
        jnp.sum(weight * spread) + jnp.sum(live_mask),
    )


def transform(perturb9, metadata9, inflation, taper, tile_x, tile_y):
    members = perturb9.shape[-1]
    bins = taper.shape[0]
    offsets = jnp.arange(3, dtype=jnp.int32) - 1
    column_pos = offsets[:, None, None] * tile_x + metadata9[:, :, 2, :].astype(jnp.int32)
    row_pos = offsets[None, :, None] * tile_y + metadata9[:, :, 3, :].astype(jnp.int32)
    delta_x = 2 * column_pos - (tile_x - 1)
    delta_y = 2 * row_pos - (tile_y - 1)
    distance = (delta_x * delta_x + delta_y * delta_y) * bins
    limit = 9 * (tile_x * tile_x + tile_y * tile_y)
    bin_edges = jnp.arange(bins, dtype=jnp.int32) * limit
    in_bin = (distance[..., None] >= bin_edges) & (distance[..., None] < bin_edges + limit)
    tapered_weight_factor = (
        jnp.sum(jnp.where(in_bin, taper.astype(jnp.float32), jnp.float32(0.0)), axis=-1) / 1024.0
    )
    effective = metadata9[:, :, 1, :].astype(jnp.float32) * tapered_weight_factor
    flat = perturb9.reshape(-1, members)
    weighted = (flat.astype(jnp.float32) * effective.reshape(-1)[:, None]).astype(jnp.bfloat16)
    gram_matrix = lax.dot_general(
        weighted, flat, (((0,), (0,)), ((), ())), preferred_element_type=jnp.float32
    )
    innovation = metadata9[:, :, 0, :].reshape(1, -1)
    projected = jnp.dot(innovation, weighted, preferred_element_type=jnp.float32)[0]
    identity = jnp.eye(members, dtype=jnp.float32)
    system = identity / inflation + gram_matrix / (members - 1)
    frobenius = jnp.sqrt(jnp.sum(system * system))
    root_iter = system / frobenius
    inverse_root = identity
    for sweep in range(NSTEPS):
        correction = 1.5 * identity - 0.5 * jnp.dot(
            inverse_root, root_iter, precision=HIGH, preferred_element_type=jnp.float32
        )
        root_iter = jnp.dot(
            root_iter, correction, precision=HIGH, preferred_element_type=jnp.float32
        )
        inverse_root = jnp.dot(
            correction, inverse_root, precision=HIGH, preferred_element_type=jnp.float32
        )
    spread_weights = inverse_root / jnp.sqrt(frobenius)
    inner = jnp.dot(inverse_root, projected, precision=HIGH, preferred_element_type=jnp.float32)
    mean_weights = jnp.dot(
        inverse_root, inner, precision=HIGH, preferred_element_type=jnp.float32
    ) / (frobenius * (members - 1))
    return (spread_weights + mean_weights[:, None]).astype(jnp.bfloat16)


def spline(length, tile_id, tiles):
    position = (jnp.arange(length, dtype=jnp.float32) + 0.5) / length
    left_part = 0.5 * jnp.square(1.0 - position)
    middle = 0.5 + position - jnp.square(position)
    right_part = 0.5 * jnp.square(position)
    has_left = (tile_id > 0).astype(jnp.float32)
    has_right = (tile_id < tiles - 1).astype(jnp.float32)
    middle = middle + (1.0 - has_left) * left_part + (1.0 - has_right) * right_part
    return jnp.stack([left_part * has_left, middle, right_part * has_right])


def blend(ensemble, weights9, column_id, row_id, columns, row_tiles):
    levels, tile_x, tile_y, members = ensemble.shape
    widened = ensemble.astype(jnp.float32)
    center = jnp.mean(widened, axis=-1, keepdims=True)
    deviation = widened - center
    beta_x = spline(tile_x, column_id, columns)
    beta_y = spline(tile_y, row_id, row_tiles)
    analysis = center
    for offset_y in range(3):
        pieces = [
            (
                deviation
                * (beta_x[offset_x][:, None] * beta_y[offset_y][None, :])[None, :, :, None]
            ).astype(jnp.bfloat16)
            for offset_x in range(3)
        ]
        stacked = jnp.concatenate(pieces, axis=-1).reshape(-1, 3 * members)
        column_stack = weights9[:, offset_y].reshape(3 * members, members)
        product = jnp.dot(stacked, column_stack, preferred_element_type=jnp.float32)
        analysis = analysis + product.reshape(levels, tile_x, tile_y, members)
    return analysis.astype(jnp.bfloat16)


def local(background, observation_cell_index, obs_value, obs_inverse, obs_count, taper):
    levels, tile_x, tile_y, members = background.shape
    slot_total = observation_cell_index.shape[2]
    ensemble = background.reshape(-1, members)
    perturb, metadata, live_mask = observe(
        ensemble,
        observation_cell_index[0, 0],
        obs_value[0, 0],
        obs_inverse[0, 0],
        obs_count[0, 0],
        tile_x,
        tile_y,
    )
    numerator, denominator = statistics(perturb, metadata, live_mask)
    numerator, denominator = lax.psum((numerator, denominator), ("gx", "gy"))
    inflation = numerator / denominator
    packed = jnp.concatenate([perturb, metadata.reshape(-1, members)], axis=0)[None, None]
    adjacent_tiles = extended(packed, (("gx", 0), ("gy", 1)), 1)
    neighbour_perturbation_rows = adjacent_tiles[:, :, :slot_total]
    neighbour_metadata_rows = adjacent_tiles[:, :, slot_total:].reshape(3, 3, 4, slot_total)
    tile_weights = transform(
        neighbour_perturbation_rows, neighbour_metadata_rows, inflation, taper, tile_x, tile_y
    )[None, None]
    near_weights = extended(tile_weights, (("gx", 0), ("gy", 1)), 1)
    return blend(
        background,
        near_weights,
        lax.axis_index("gx"),
        lax.axis_index("gy"),
        lax.axis_size("gx"),
        lax.axis_size("gy"),
    )


def solution(mesh):
    in_specs = (
        P(None, "gx", "gy", None),
        P("gx", "gy", None),
        P("gx", "gy", None),
        P("gx", "gy", None),
        P("gx", "gy"),
        P(),
    )
    out_specs = P(None, "gx", "gy", None)
    return jax.shard_map(local, mesh=mesh, in_specs=in_specs, out_specs=out_specs, check_vma=False)
```

profile of v0, /device:TPU:2, one launch (start us, length us, event | category | flops | bytes accessed | tf_op | source)
XLA Modules:
  0.0 185.3 jit_solution(1450910014959891026)
XLA Ops:
  0.0 0.0 copy-start
  0.0 0.7 fusion.60
  0.7 0.7 compare_select_fusion
  2.1 0.7 compare_and_fusion
  2.8 3.8 %gather_fusion = bf16[512,128]{1,0:T(8,128)(2,1)S(1)} fusion(bf16[16384,128]{1,0:T(8,128)(2,1)} %bitcast.130, s32[1024]{0:T(1024)S(1)} %pad_clamp_fusion), kind=kCustom, calls=%fused_computation | custom fusion | bytes 264192 | tf_op jit(solution)/shard_map/jit(_take)/gather | solution.py:28
  6.6 0.2 convert_reduce_fusion.1
  6.8 0.3 multiply_reduce_fusion
  7.1 0.7 compare_select_fusion.1
  7.9 1.3 collective-permute-start.1
  9.2 3.0 %collective-permute-start = (bf16[1,1,528,128]{3,2,1,0:T(8,128)(2,1)S(1)}, bf16[1,1,528,128]{3,2,1,0:T(8,128)(2,1)S(1)}, u32[]{:S(2)}, u32[]{:S(2)}) collective-permute-start(bf16[1,1,528,128]{3,2,1,0:T(8,128)(2,1)S(1)} %maximum_bitcast_fusion), channel_id=1, source_target_pairs={{0,8},{8,16},{16,24},{24,32},{32,40},{40,48},{48,56},{56,64},{64,7... | collective-permute-start | bytes 405512 | tf_op jit(solution)/shard_map/ppermute | solution.py:18
  12.3 3.4 %convert_reduce_fusion = f32[2,64,128]{2,1,0:T(8,128)S(1)} fusion(bf16[2,64,128,128]{3,2,1,0:T(8,128)(2,1)} %param.6), kind=kLoop, calls=%fused_computation.20 | loop fusion | flops 4177920 | bytes 4259840 | tf_op jit(solution)/shard_map/reduce_sum | solution.py:117
  15.7 0.7 fusion.58
  16.4 0.6 convert_reduce_fusion.2
  18.2 83.2 %all-reduce = (f32[]{:T(128)}, f32[]{:T(128)}) all-reduce(f32[]{:T(128)S(6)} %add.238, f32[]{:T(128)} %get-tuple-element.5), channel_id=1, replica_groups=mesh['gx'=32,'gy'=8] {'gx','gy'}, use_global_device_ids=true, to_apply=%region_5.6 | all-reduce | flops 2 | bytes 16 | tf_op jit(solution)/shard_map/psum | solution.py:151
  101.4 0.0 copy-done
  102.7 0.0 collective-permute-done.1
  102.7 0.0 collective-permute-done
  102.8 4.6 %collective-permute-start.3 = (bf16[3,1,528,128]{3,2,1,0:T(8,128)(2,1)S(1)}, bf16[3,1,528,128]{3,2,1,0:T(8,128)(2,1)S(1)}, u32[]{:S(2)}, u32[]{:S(2)}) collective-permute-start(bf16[3,1,528,128]{3,2,1,0:T(8,128)(2,1)S(1)} %pad_maximum_fusion.1), channel_id=1, source_target_pairs={{1,0},{2,1},{3,2},{4,3},{5,4},{6,5},{7,6},{9,8},{10,9},{11,10},{12... | collective-permute-start | bytes 1216520 | tf_op jit(solution)/shard_map/ppermute | solution.py:20
  107.4 1.9 %collective-permute-start.2 = (bf16[3,1,528,128]{3,2,1,0:T(8,128)(2,1)S(1)}, bf16[3,1,528,128]{3,2,1,0:T(8,128)(2,1)S(1)}, u32[]{:S(2)}, u32[]{:S(2)}) collective-permute-start(bf16[3,1,528,128]{3,2,1,0:T(8,128)(2,1)S(1)} %pad_maximum_fusion.1), channel_id=1, source_target_pairs={{0,1},{1,2},{2,3},{3,4},{4,5},{5,6},{6,7},{8,9},{9,10},{10,11},{11... | collective-permute-start | bytes 1216520 | tf_op jit(solution)/shard_map/ppermute | solution.py:18
  109.3 0.1 broadcast_multiply_fusion.3
  109.4 6.6 %collective-permute-done.3 = bf16[3,1,528,128]{3,2,1,0:T(8,128)(2,1)S(1)} collective-permute-done((bf16[3,1,528,128]{3,2,1,0:T(8,128)(2,1)S(1)}, bf16[3,1,528,128]{3,2,1,0:T(8,128)(2,1)S(1)}, u32[]{:S(2)}, u32[]{:S(2)}) %collective-permute-start.3) | collective-permute-done | bytes 405536 | tf_op jit(solution)/shard_map/ppermute | solution.py:20
  116.0 6.2 %collective-permute-done.2 = bf16[3,1,528,128]{3,2,1,0:T(8,128)(2,1)S(1)} collective-permute-done((bf16[3,1,528,128]{3,2,1,0:T(8,128)(2,1)S(1)}, bf16[3,1,528,128]{3,2,1,0:T(8,128)(2,1)S(1)}, u32[]{:S(2)}, u32[]{:S(2)}) %collective-permute-start.2) | collective-permute-done | bytes 405536 | tf_op jit(solution)/shard_map/ppermute | solution.py:18
  122.2 0.1 fusion.71
  122.3 0.1 fusion.54
  122.4 0.3 select_reduce_fusion
  122.7 0.1 pad_maximum_fusion
  122.9 0.8 multiply_convert_fusion
  123.7 1.1 multiply_reduce_fusion.1
  125.5 0.2 fusion.41
  125.7 0.2 fusion.47
  125.9 0.2 fusion.49
  126.1 0.2 fusion.40
  126.3 0.2 fusion.72
  126.5 0.2 fusion.73
  126.7 0.2 fusion.39
  127.0 0.2 fusion.74
  127.2 0.2 fusion.75
  127.4 0.2 fusion.38
  127.6 0.2 fusion.76
  127.8 0.2 fusion.77
  128.0 0.2 fusion.37
  128.2 0.2 fusion.78
  128.4 0.2 fusion.79
  128.7 0.2 fusion.36
  128.9 0.2 fusion.80
  129.1 0.3 convolution_bitcast_fusion.3
  129.4 0.2 convolution_bitcast_fusion.2
  129.6 0.2 fusion.44
  129.8 0.1 fusion.48
  129.9 1.3 collective-permute-start.5
  131.2 3.0 %collective-permute-start.4 = (bf16[1,1,128,128]{3,2,1,0:T(8,128)(2,1)S(1)}, bf16[1,1,128,128]{3,2,1,0:T(8,128)(2,1)S(1)}, u32[]{:S(2)}, u32[]{:S(2)}) collective-permute-start(bf16[1,1,128,128]{3,2,1,0:T(8,128)(2,1)S(1)} %fusion.48), channel_id=1, source_target_pairs={{0,8},{8,16},{16,24},{24,32},{32,40},{40,48},{48,56},{56,64},{64,7... | collective-permute-start | bytes 98312 | tf_op jit(solution)/shard_map/ppermute | solution.py:18
  134.3 17.4 %fusion.33 = (bf16[2,64,128,128]{3,2,1,0:T(8,128)(2,1)S(1)}, bf16[2,64,128,128]{3,2,1,0:T(8,128)(2,1)S(1)}, bf16[2,64,128,128]{3,2,1,0:T(8,128)(2,1)S(1)}, bf16[...) fusion(bf16[2,64,128,128]{3,2,1,0:T(8,128)(2,1)} %param.6, ...), kind=kLoop, calls=%fused_computation.36 | loop fusion | flops 41943040 | bytes 42303488 | tf_op jit(solution)/shard_map/convert_element_type | solution.py:127
  151.6 0.0 collective-permute-done.5
  151.6 0.0 collective-permute-done.4
  151.7 1.9 %collective-permute-start.6 = (bf16[3,1,128,128]{3,2,1,0:T(8,128)(2,1)S(1)}, bf16[3,1,128,128]{3,2,1,0:T(8,128)(2,1)S(1)}, u32[]{:S(2)}, u32[]{:S(2)}) collective-permute-start(bf16[3,1,128,128]{3,2,1,0:T(8,128)(2,1)S(1)} %pad_maximum_fusion.2), channel_id=1, source_target_pairs={{0,1},{1,2},{2,3},{3,4},{4,5},{5,6},{6,7},{8,9},{9,10},{10,11},{11... | collective-permute-start | bytes 294920 | tf_op jit(solution)/shard_map/ppermute | solution.py:18
  153.6 6.0 %collective-permute-start.7 = (bf16[3,1,128,128]{3,2,1,0:T(8,128)(2,1)S(1)}, bf16[3,1,128,128]{3,2,1,0:T(8,128)(2,1)S(1)}, u32[]{:S(2)}, u32[]{:S(2)}) collective-permute-start(bf16[3,1,128,128]{3,2,1,0:T(8,128)(2,1)S(1)} %pad_maximum_fusion.2), channel_id=1, source_target_pairs={{1,0},{2,1},{3,2},{4,3},{5,4},{6,5},{7,6},{9,8},{10,9},{11,10},{12... | collective-permute-start | bytes 294920 | tf_op jit(solution)/shard_map/ppermute | solution.py:20
  159.6 8.5 %fusion.6 = f32[2,64,128,128]{3,2,1,0:T(8,128)} fusion(bf16[384,128,1,1]{1,0,3,2:T(8,128)(2,1)S(1)} %bitcast.132, bf16[2,64,128,128]{3,2,1,0:T(8,128)(2,1)} %get-tuple-element.16, bf16[2,64,128,128]{3,2,1,0:T(8,128)(2,1)} %get-tuple-element.15, bf16[2,64,128,128]{3,2,1,0:T(8,128)(2,1)} %get-tuple-element.14), kind=kOutput, calls=%fused_computation.7 | convolution fusion | flops 1648361472 | bytes 21069824 | tf_op jit(solution)/shard_map/dot_general | solution.py:132
  168.1 0.0 collective-permute-done.6
  168.1 5.7 %fusion = f32[2,64,128,128]{3,2,1,0:T(8,128)} fusion(bf16[384,128,1,1]{1,0,3,2:T(8,128)(2,1)S(1)} %bitcast.140, bf16[2,64,128,128]{3,2,1,0:T(8,128)(2,1)S(1)} %get-tuple-element.13, bf16[2,64,128,128]{3,2,1,0:T(8,128)(2,1)S(1)} %get-tuple-element.12, bf16[2,64,128,128]{3,2,1,0:T(8,128)(2,1)S(1)} %get-tuple-element.19), kind=kOutput, calls=%fused_computation.1 | convolution fusion | flops 1648361472 | bytes 21069824 | tf_op jit(solution)/shard_map/dot_general | solution.py:132
  173.8 0.0 collective-permute-done.7
  173.8 11.4 %add_convert_fusion = bf16[2,64,128,128]{3,2,1,0:T(8,128)(2,1)} fusion(f32[2,64,128,128]{3,2,1,0:T(8,128)} %fusion.6, f32[2,64,128,128]{3,2,1,0:T(8,128)} %fusion, f32[2,64,128]{2,1,0:T(8,128)S(1)} %broadcast_multiply_fusion, bf16[384,128,1,1]{1,0,3,2:T(8,128)(2,1)S(1)} %bitcast.139, bf16[2,64,128,128]{3,2,1,0:T(8,128)(2,1)S(1)} %get-tuple-element.18, ...), kind=kOutput, calls=%fused_computation.39 | convolution fusion | flops 1656750080 | bytes 33718272 | tf_op jit(solution)/shard_map/dot_general | solution.py:132
  (19 shorter events, 0.2 us)
Async XLA Ops:
  0.0 101.4 %copy-start = (s32[64]{0:T(128)S(1)}, s32[64]{0:T(128)}, u32[]{:S(2)}) copy-start(s32[64]{0:T(128)} %param.11) | copy-start | bytes 772
  7.9 94.9 %collective-permute-start.1 = (bf16[1,1,528,128]{3,2,1,0:T(8,128)(2,1)S(1)}, bf16[1,1,528,128]{3,2,1,0:T(8,128)(2,1)S(1)}, u32[]{:S(2)}, u32[]{:S(2)}) collective-permute-start(bf16[1,1,528,128]{3,2,1,0:T(8,128)(2,1)S(1)} %maximum_bitcast_fusion), channel_id=1, source_target_pairs={{8,0},{16,8},{24,16},{32,24},{40,32},{48,40},{56,48},{64,56},{72,6... | collective-permute-start | bytes 405512 | tf_op jit(solution)/shard_map/ppermute | solution.py:20
  9.2 93.6 %collective-permute-start = (bf16[1,1,528,128]{3,2,1,0:T(8,128)(2,1)S(1)}, bf16[1,1,528,128]{3,2,1,0:T(8,128)(2,1)S(1)}, u32[]{:S(2)}, u32[]{:S(2)}) collective-permute-start(bf16[1,1,528,128]{3,2,1,0:T(8,128)(2,1)S(1)} %maximum_bitcast_fusion), channel_id=1, source_target_pairs={{0,8},{8,16},{16,24},{24,32},{32,40},{40,48},{48,56},{56,64},{64,7... | collective-permute-start | bytes 405512 | tf_op jit(solution)/shard_map/ppermute | solution.py:18
  102.8 13.2 %collective-permute-start.3 = (bf16[3,1,528,128]{3,2,1,0:T(8,128)(2,1)S(1)}, bf16[3,1,528,128]{3,2,1,0:T(8,128)(2,1)S(1)}, u32[]{:S(2)}, u32[]{:S(2)}) collective-permute-start(bf16[3,1,528,128]{3,2,1,0:T(8,128)(2,1)S(1)} %pad_maximum_fusion.1), channel_id=1, source_target_pairs={{1,0},{2,1},{3,2},{4,3},{5,4},{6,5},{7,6},{9,8},{10,9},{11,10},{12... | collective-permute-start | bytes 1216520 | tf_op jit(solution)/shard_map/ppermute | solution.py:20
  107.4 14.8 %collective-permute-start.2 = (bf16[3,1,528,128]{3,2,1,0:T(8,128)(2,1)S(1)}, bf16[3,1,528,128]{3,2,1,0:T(8,128)(2,1)S(1)}, u32[]{:S(2)}, u32[]{:S(2)}) collective-permute-start(bf16[3,1,528,128]{3,2,1,0:T(8,128)(2,1)S(1)} %pad_maximum_fusion.1), channel_id=1, source_target_pairs={{0,1},{1,2},{2,3},{3,4},{4,5},{5,6},{6,7},{8,9},{9,10},{10,11},{11... | collective-permute-start | bytes 1216520 | tf_op jit(solution)/shard_map/ppermute | solution.py:18
  129.9 21.7 %collective-permute-start.5 = (bf16[1,1,128,128]{3,2,1,0:T(8,128)(2,1)S(1)}, bf16[1,1,128,128]{3,2,1,0:T(8,128)(2,1)S(1)}, u32[]{:S(2)}, u32[]{:S(2)}) collective-permute-start(bf16[1,1,128,128]{3,2,1,0:T(8,128)(2,1)S(1)} %fusion.48), channel_id=1, source_target_pairs={{8,0},{16,8},{24,16},{32,24},{40,32},{48,40},{56,48},{64,56},{72,6... | collective-permute-start | bytes 98312 | tf_op jit(solution)/shard_map/ppermute | solution.py:20
  131.2 20.4 %collective-permute-start.4 = (bf16[1,1,128,128]{3,2,1,0:T(8,128)(2,1)S(1)}, bf16[1,1,128,128]{3,2,1,0:T(8,128)(2,1)S(1)}, u32[]{:S(2)}, u32[]{:S(2)}) collective-permute-start(bf16[1,1,128,128]{3,2,1,0:T(8,128)(2,1)S(1)} %fusion.48), channel_id=1, source_target_pairs={{0,8},{8,16},{16,24},{24,32},{32,40},{40,48},{48,56},{56,64},{64,7... | collective-permute-start | bytes 98312 | tf_op jit(solution)/shard_map/ppermute | solution.py:18
  151.7 16.5 %collective-permute-start.6 = (bf16[3,1,128,128]{3,2,1,0:T(8,128)(2,1)S(1)}, bf16[3,1,128,128]{3,2,1,0:T(8,128)(2,1)S(1)}, u32[]{:S(2)}, u32[]{:S(2)}) collective-permute-start(bf16[3,1,128,128]{3,2,1,0:T(8,128)(2,1)S(1)} %pad_maximum_fusion.2), channel_id=1, source_target_pairs={{0,1},{1,2},{2,3},{3,4},{4,5},{5,6},{6,7},{8,9},{9,10},{10,11},{11... | collective-permute-start | bytes 294920 | tf_op jit(solution)/shard_map/ppermute | solution.py:18
  153.6 20.2 %collective-permute-start.7 = (bf16[3,1,128,128]{3,2,1,0:T(8,128)(2,1)S(1)}, bf16[3,1,128,128]{3,2,1,0:T(8,128)(2,1)S(1)}, u32[]{:S(2)}, u32[]{:S(2)}) collective-permute-start(bf16[3,1,128,128]{3,2,1,0:T(8,128)(2,1)S(1)} %pad_maximum_fusion.2), channel_id=1, source_target_pairs={{1,0},{2,1},{3,2},{4,3},{5,4},{6,5},{7,6},{9,8},{10,9},{11,10},{12... | collective-permute-start | bytes 294920 | tf_op jit(solution)/shard_map/ppermute | solution.py:20
where the time goes:
time: 186 us; the launch traced here: 185 us
  blocking collectives  83.2 us (45%)
  matrix products  30.8 us (17%)
  other arithmetic  27.2 us (15%)
  starting transfers between devices  23.1 us (12%)
  waiting for transfers between devices  12.8 us (7%)
  between operations  4.26 us (2%)
  local copies, waits for them, and re-layouts  3.82 us (2%)
    psum x1, blocking collectives, local(): numerator, denominator = lax.psum((numerator, denominator), ('gx', 'gy'))  83.2 us
    dot_general x3, matrix products, blend(): product = jnp.dot(stacked, column_stack, preferred_element_type=jnp.float32)  25.6 us
    convert_element_type x1, other arithmetic, blend(): pieces = [(deviation * (beta_x[offset_x][:, None] * beta_y[offset_y][None...  17.4 us
    ppermute x4, starting transfers between devices, extended(): lax.ppermute(head, axis, [((i + 1) % count, i) for i in range(ends)])  13.2 us
    ppermute x4, starting transfers between devices, extended(): lax.ppermute(tail, axis, [(i, (i + 1) % count) for i in range(ends)])  9.91 us
    ppermute x4, waiting for transfers between devices, extended(): lax.ppermute(head, axis, [((i + 1) % count, i) for i in range(ends)])  6.56 us
    ppermute x4, waiting for transfers between devices, extended(): lax.ppermute(tail, axis, [(i, (i + 1) % count) for i in range(ends)])  6.23 us
    gather x1, local copies, waits for them, and re-layouts, observe(): picked = jnp.take(ensemble, cell_ids, axis=0).astype(jnp.float32)  3.78 us
  transfers between devices with their start and end apart: 8, of which 2 were waited for; matrix products, arithmetic and copies ran while one was open for 20% of the time, Pallas kernels for 0%

commit v1 on v0

--- a/solution.py
+++ b/solution.py
@@ -148,7 +148,7 @@
         tile_y,
     )
     numerator, denominator = statistics(perturb, metadata, live_mask)
-    numerator, denominator = lax.psum((numerator, denominator), ("gx", "gy"))
+    numerator, denominator = jax.lax.psum(jax.lax.psum((numerator, denominator), "gy"), "gx")
     inflation = numerator / denominator
     packed = jnp.concatenate([perturb, metadata.reshape(-1, members)], axis=0)[None, None]
     adjacent_tiles = extended(packed, (("gx", 0), ("gy", 1)), 1)

time: 186 us -> 191 us (1.027); the launches traced: 185 us -> 188 us
  blocking collectives: 83.2 us -> 88.1 us
  waiting for transfers between devices: 12.8 us -> 10.7 us
    psum x1 -> x2, blocking collectives: 83.2 us -> 88.1 us  [the longest x1 68.3 us: local(): jax.lax.psum(jax.lax.psum((numerator, denominator), 'gy'), 'gx')]
    ppermute x4, waiting for transfers between devices: 6.23 us -> 4.11 us  [extended(): lax.ppermute(tail, axis, [(i, (i + 1) % count) for i in range(ends)])]
    ppermute x4, starting transfers between devices: 13.2 us -> 11.2 us  [extended(): lax.ppermute(head, axis, [((i + 1) % count, i) for i in range(ends)])]
  transfers between devices with their start and end apart: 8 -> 8, of which waited for: 2 -> 2; matrix products, arithmetic and copies ran while one was open for 20% -> 19% of each run, Pallas kernels for 0% -> 0%
where the time goes in v1:
time: 191 us; the launch traced here: 188 us
  blocking collectives  88.1 us (46%)
  matrix products  30.8 us (16%)
  other arithmetic  27.2 us (14%)
  starting transfers between devices  22.4 us (12%)
  waiting for transfers between devices  10.7 us (6%)
  between operations  4.39 us (2%)
  local copies, waits for them, and re-layouts  3.82 us (2%)
    psum x1, blocking collectives, local(): jax.lax.psum(jax.lax.psum((numerator, denominator), 'gy'), 'gx')  68.3 us
    dot_general x3, matrix products, blend(): product = jnp.dot(stacked, column_stack, preferred_element_type=jnp.float32)  25.6 us
    psum x1, blocking collectives, local(): jax.lax.psum((numerator, denominator), 'gy')  19.8 us
    convert_element_type x1, other arithmetic, blend(): pieces = [(deviation * (beta_x[offset_x][:, None] * beta_y[offset_y][None...  17.4 us
    ppermute x4, starting transfers between devices, extended(): lax.ppermute(tail, axis, [(i, (i + 1) % count) for i in range(ends)])  11.3 us
    ppermute x4, starting transfers between devices, extended(): lax.ppermute(head, axis, [((i + 1) % count, i) for i in range(ends)])  11.2 us
    ppermute x4, waiting for transfers between devices, extended(): lax.ppermute(head, axis, [((i + 1) % count, i) for i in range(ends)])  6.64 us
    ppermute x4, waiting for transfers between devices, extended(): lax.ppermute(tail, axis, [(i, (i + 1) % count) for i in range(ends)])  4.11 us
  transfers between devices with their start and end apart: 8, of which 2 were waited for; matrix products, arithmetic and copies ran while one was open for 19% of the time, Pallas kernels for 0%

profile of v1, /device:TPU:2, one launch (start us, length us, event | category | flops | bytes accessed | tf_op | source)
XLA Modules:
  0.0 187.5 jit_solution(1732813800015669945)
XLA Ops:
  0.0 0.0 copy-start
  0.0 0.7 fusion.60
  0.7 0.7 compare_select_fusion
  2.1 0.7 compare_and_fusion
  2.8 3.8 %gather_fusion = bf16[512,128]{1,0:T(8,128)(2,1)S(1)} fusion(bf16[16384,128]{1,0:T(8,128)(2,1)} %bitcast.130, s32[1024]{0:T(1024)S(1)} %pad_clamp_fusion), kind=kCustom, calls=%fused_computation | custom fusion | bytes 264192 | tf_op jit(solution)/shard_map/jit(_take)/gather | solution.py:28
  6.6 0.2 convert_reduce_fusion.1
  6.8 0.3 multiply_reduce_fusion
  7.1 0.7 compare_select_fusion.1
  7.9 1.3 collective-permute-start.1
  9.2 3.0 %collective-permute-start = (bf16[1,1,528,128]{3,2,1,0:T(8,128)(2,1)S(1)}, bf16[1,1,528,128]{3,2,1,0:T(8,128)(2,1)S(1)}, u32[]{:S(2)}, u32[]{:S(2)}) collective-permute-start(bf16[1,1,528,128]{3,2,1,0:T(8,128)(2,1)S(1)} %maximum_bitcast_fusion), channel_id=1, source_target_pairs={{0,8},{8,16},{16,24},{24,32},{32,40},{40,48},{48,56},{56,64},{64,7... | collective-permute-start | bytes 405512 | tf_op jit(solution)/shard_map/ppermute | solution.py:18
  12.3 3.4 %convert_reduce_fusion = f32[2,64,128]{2,1,0:T(8,128)S(1)} fusion(bf16[2,64,128,128]{3,2,1,0:T(8,128)(2,1)} %param.6), kind=kLoop, calls=%fused_computation.20 | loop fusion | flops 4177920 | bytes 4259840 | tf_op jit(solution)/shard_map/reduce_sum | solution.py:117
  15.7 0.7 fusion.58
  16.4 0.6 convert_reduce_fusion.2
  18.2 19.8 %all-reduce.1 = (f32[]{:T(128)}, f32[]{:T(128)}) all-reduce(f32[]{:T(128)S(6)} %add.242, f32[]{:T(128)} %get-tuple-element.5), channel_id=1, replica_groups=mesh['gx'=32,'gy'=8] {'gy'}, use_global_device_ids=true, to_apply=%region_5.6 | all-reduce | flops 2 | bytes 16 | tf_op jit(solution)/shard_map/psum | solution.py:151
  38.0 68.3 %all-reduce = (f32[]{:T(128)}, f32[]{:T(128)}) all-reduce(f32[]{:T(128)} %get-tuple-element.9, f32[]{:T(128)} %get-tuple-element.10), channel_id=1, replica_groups=mesh['gx'=32,'gy'=8] {'gx'}, use_global_device_ids=true, to_apply=%region_6.7 | all-reduce | flops 2 | bytes 16 | tf_op jit(solution)/shard_map/psum | solution.py:151
  106.3 0.0 copy-done
  107.7 0.0 collective-permute-done.1
  107.7 0.0 collective-permute-done
  107.8 2.6 %collective-permute-start.3 = (bf16[3,1,528,128]{3,2,1,0:T(8,128)(2,1)S(1)}, bf16[3,1,528,128]{3,2,1,0:T(8,128)(2,1)S(1)}, u32[]{:S(2)}, u32[]{:S(2)}) collective-permute-start(bf16[3,1,528,128]{3,2,1,0:T(8,128)(2,1)S(1)} %pad_maximum_fusion.1), channel_id=1, source_target_pairs={{1,0},{2,1},{3,2},{4,3},{5,4},{6,5},{7,6},{9,8},{10,9},{11,10},{12... | collective-permute-start | bytes 1216520 | tf_op jit(solution)/shard_map/ppermute | solution.py:20
  110.3 3.3 %collective-permute-start.2 = (bf16[3,1,528,128]{3,2,1,0:T(8,128)(2,1)S(1)}, bf16[3,1,528,128]{3,2,1,0:T(8,128)(2,1)S(1)}, u32[]{:S(2)}, u32[]{:S(2)}) collective-permute-start(bf16[3,1,528,128]{3,2,1,0:T(8,128)(2,1)S(1)} %pad_maximum_fusion.1), channel_id=1, source_target_pairs={{0,1},{1,2},{2,3},{3,4},{4,5},{5,6},{6,7},{8,9},{9,10},{10,11},{11... | collective-permute-start | bytes 1216520 | tf_op jit(solution)/shard_map/ppermute | solution.py:18
  113.7 0.1 broadcast_multiply_fusion.3
  113.8 6.6 %collective-permute-done.3 = bf16[3,1,528,128]{3,2,1,0:T(8,128)(2,1)S(1)} collective-permute-done((bf16[3,1,528,128]{3,2,1,0:T(8,128)(2,1)S(1)}, bf16[3,1,528,128]{3,2,1,0:T(8,128)(2,1)S(1)}, u32[]{:S(2)}, u32[]{:S(2)}) %collective-permute-start.3) | collective-permute-done | bytes 405536 | tf_op jit(solution)/shard_map/ppermute | solution.py:20
  120.4 4.1 %collective-permute-done.2 = bf16[3,1,528,128]{3,2,1,0:T(8,128)(2,1)S(1)} collective-permute-done((bf16[3,1,528,128]{3,2,1,0:T(8,128)(2,1)S(1)}, bf16[3,1,528,128]{3,2,1,0:T(8,128)(2,1)S(1)}, u32[]{:S(2)}, u32[]{:S(2)}) %collective-permute-start.2) | collective-permute-done | bytes 405536 | tf_op jit(solution)/shard_map/ppermute | solution.py:18
  124.5 0.1 fusion.71
  124.6 0.1 fusion.54
  124.7 0.3 select_reduce_fusion
  125.0 0.1 pad_maximum_fusion
  125.2 0.8 multiply_convert_fusion
  126.0 1.1 multiply_reduce_fusion.1
  127.8 0.2 fusion.41
  128.0 0.2 fusion.47
  128.2 0.2 fusion.49
  128.4 0.2 fusion.40
  128.6 0.2 fusion.72
  128.8 0.2 fusion.73
  129.0 0.2 fusion.39
  129.2 0.2 fusion.74
  129.4 0.2 fusion.75
  129.6 0.2 fusion.38
  129.9 0.2 fusion.76
  130.1 0.2 fusion.77
  130.3 0.2 fusion.37
  130.5 0.2 fusion.78
  130.7 0.2 fusion.79
  131.0 0.2 fusion.36
  131.2 0.2 fusion.80
  131.4 0.3 convolution_bitcast_fusion.3
  131.6 0.2 convolution_bitcast_fusion.2
  131.8 0.2 fusion.44
  132.1 0.1 fusion.48
  132.2 1.3 collective-permute-start.5
  133.5 3.0 %collective-permute-start.4 = (bf16[1,1,128,128]{3,2,1,0:T(8,128)(2,1)S(1)}, bf16[1,1,128,128]{3,2,1,0:T(8,128)(2,1)S(1)}, u32[]{:S(2)}, u32[]{:S(2)}) collective-permute-start(bf16[1,1,128,128]{3,2,1,0:T(8,128)(2,1)S(1)} %fusion.48), channel_id=1, source_target_pairs={{0,8},{8,16},{16,24},{24,32},{32,40},{40,48},{48,56},{56,64},{64,7... | collective-permute-start | bytes 98312 | tf_op jit(solution)/shard_map/ppermute | solution.py:18
  136.5 17.4 %fusion.33 = (bf16[2,64,128,128]{3,2,1,0:T(8,128)(2,1)S(1)}, bf16[2,64,128,128]{3,2,1,0:T(8,128)(2,1)S(1)}, bf16[2,64,128,128]{3,2,1,0:T(8,128)(2,1)S(1)}, bf16[...) fusion(bf16[2,64,128,128]{3,2,1,0:T(8,128)(2,1)} %param.6, ...), kind=kLoop, calls=%fused_computation.36 | loop fusion | flops 41943040 | bytes 42303488 | tf_op jit(solution)/shard_map/convert_element_type | solution.py:127
  153.9 0.0 collective-permute-done.5
  153.9 0.0 collective-permute-done.4
  153.9 1.9 %collective-permute-start.6 = (bf16[3,1,128,128]{3,2,1,0:T(8,128)(2,1)S(1)}, bf16[3,1,128,128]{3,2,1,0:T(8,128)(2,1)S(1)}, u32[]{:S(2)}, u32[]{:S(2)}) collective-permute-start(bf16[3,1,128,128]{3,2,1,0:T(8,128)(2,1)S(1)} %pad_maximum_fusion.2), channel_id=1, source_target_pairs={{0,1},{1,2},{2,3},{3,4},{4,5},{5,6},{6,7},{8,9},{9,10},{10,11},{11... | collective-permute-start | bytes 294920 | tf_op jit(solution)/shard_map/ppermute | solution.py:18
  155.9 6.0 %collective-permute-start.7 = (bf16[3,1,128,128]{3,2,1,0:T(8,128)(2,1)S(1)}, bf16[3,1,128,128]{3,2,1,0:T(8,128)(2,1)S(1)}, u32[]{:S(2)}, u32[]{:S(2)}) collective-permute-start(bf16[3,1,128,128]{3,2,1,0:T(8,128)(2,1)S(1)} %pad_maximum_fusion.2), channel_id=1, source_target_pairs={{1,0},{2,1},{3,2},{4,3},{5,4},{6,5},{7,6},{9,8},{10,9},{11,10},{12... | collective-permute-start | bytes 294920 | tf_op jit(solution)/shard_map/ppermute | solution.py:20
  161.9 8.5 %fusion.6 = f32[2,64,128,128]{3,2,1,0:T(8,128)} fusion(bf16[384,128,1,1]{1,0,3,2:T(8,128)(2,1)S(1)} %bitcast.132, bf16[2,64,128,128]{3,2,1,0:T(8,128)(2,1)} %get-tuple-element.18, bf16[2,64,128,128]{3,2,1,0:T(8,128)(2,1)} %get-tuple-element.17, bf16[2,64,128,128]{3,2,1,0:T(8,128)(2,1)} %get-tuple-element.16), kind=kOutput, calls=%fused_computation.7 | convolution fusion | flops 1648361472 | bytes 21069824 | tf_op jit(solution)/shard_map/dot_general | solution.py:132
  170.4 0.0 collective-permute-done.6
  170.4 5.7 %fusion = f32[2,64,128,128]{3,2,1,0:T(8,128)} fusion(bf16[384,128,1,1]{1,0,3,2:T(8,128)(2,1)S(1)} %bitcast.140, bf16[2,64,128,128]{3,2,1,0:T(8,128)(2,1)S(1)} %get-tuple-element.15, bf16[2,64,128,128]{3,2,1,0:T(8,128)(2,1)S(1)} %get-tuple-element.14, bf16[2,64,128,128]{3,2,1,0:T(8,128)(2,1)S(1)} %get-tuple-element.21), kind=kOutput, calls=%fused_computation.1 | convolution fusion | flops 1648361472 | bytes 21069824 | tf_op jit(solution)/shard_map/dot_general | solution.py:132
  176.1 0.0 collective-permute-done.7
  176.1 11.4 %add_convert_fusion = bf16[2,64,128,128]{3,2,1,0:T(8,128)(2,1)} fusion(f32[2,64,128,128]{3,2,1,0:T(8,128)} %fusion.6, f32[2,64,128,128]{3,2,1,0:T(8,128)} %fusion, f32[2,64,128]{2,1,0:T(8,128)S(1)} %broadcast_multiply_fusion, bf16[384,128,1,1]{1,0,3,2:T(8,128)(2,1)S(1)} %bitcast.139, bf16[2,64,128,128]{3,2,1,0:T(8,128)(2,1)S(1)} %get-tuple-element.20, ...), kind=kOutput, calls=%fused_computation.39 | convolution fusion | flops 1656750080 | bytes 33718272 | tf_op jit(solution)/shard_map/dot_general | solution.py:132
  (19 shorter events, 0.2 us)
Async XLA Ops:
  0.0 106.3 %copy-start = (s32[64]{0:T(128)S(1)}, s32[64]{0:T(128)}, u32[]{:S(2)}) copy-start(s32[64]{0:T(128)} %param.11) | copy-start | bytes 772
  7.9 99.8 %collective-permute-start.1 = (bf16[1,1,528,128]{3,2,1,0:T(8,128)(2,1)S(1)}, bf16[1,1,528,128]{3,2,1,0:T(8,128)(2,1)S(1)}, u32[]{:S(2)}, u32[]{:S(2)}) collective-permute-start(bf16[1,1,528,128]{3,2,1,0:T(8,128)(2,1)S(1)} %maximum_bitcast_fusion), channel_id=1, source_target_pairs={{8,0},{16,8},{24,16},{32,24},{40,32},{48,40},{56,48},{64,56},{72,6... | collective-permute-start | bytes 405512 | tf_op jit(solution)/shard_map/ppermute | solution.py:20
  9.2 98.5 %collective-permute-start = (bf16[1,1,528,128]{3,2,1,0:T(8,128)(2,1)S(1)}, bf16[1,1,528,128]{3,2,1,0:T(8,128)(2,1)S(1)}, u32[]{:S(2)}, u32[]{:S(2)}) collective-permute-start(bf16[1,1,528,128]{3,2,1,0:T(8,128)(2,1)S(1)} %maximum_bitcast_fusion), channel_id=1, source_target_pairs={{0,8},{8,16},{16,24},{24,32},{32,40},{40,48},{48,56},{56,64},{64,7... | collective-permute-start | bytes 405512 | tf_op jit(solution)/shard_map/ppermute | solution.py:18
  107.8 12.6 %collective-permute-start.3 = (bf16[3,1,528,128]{3,2,1,0:T(8,128)(2,1)S(1)}, bf16[3,1,528,128]{3,2,1,0:T(8,128)(2,1)S(1)}, u32[]{:S(2)}, u32[]{:S(2)}) collective-permute-start(bf16[3,1,528,128]{3,2,1,0:T(8,128)(2,1)S(1)} %pad_maximum_fusion.1), channel_id=1, source_target_pairs={{1,0},{2,1},{3,2},{4,3},{5,4},{6,5},{7,6},{9,8},{10,9},{11,10},{12... | collective-permute-start | bytes 1216520 | tf_op jit(solution)/shard_map/ppermute | solution.py:20
  110.3 14.1 %collective-permute-start.2 = (bf16[3,1,528,128]{3,2,1,0:T(8,128)(2,1)S(1)}, bf16[3,1,528,128]{3,2,1,0:T(8,128)(2,1)S(1)}, u32[]{:S(2)}, u32[]{:S(2)}) collective-permute-start(bf16[3,1,528,128]{3,2,1,0:T(8,128)(2,1)S(1)} %pad_maximum_fusion.1), channel_id=1, source_target_pairs={{0,1},{1,2},{2,3},{3,4},{4,5},{5,6},{6,7},{8,9},{9,10},{10,11},{11... | collective-permute-start | bytes 1216520 | tf_op jit(solution)/shard_map/ppermute | solution.py:18
  132.2 21.7 %collective-permute-start.5 = (bf16[1,1,128,128]{3,2,1,0:T(8,128)(2,1)S(1)}, bf16[1,1,128,128]{3,2,1,0:T(8,128)(2,1)S(1)}, u32[]{:S(2)}, u32[]{:S(2)}) collective-permute-start(bf16[1,1,128,128]{3,2,1,0:T(8,128)(2,1)S(1)} %fusion.48), channel_id=1, source_target_pairs={{8,0},{16,8},{24,16},{32,24},{40,32},{48,40},{56,48},{64,56},{72,6... | collective-permute-start | bytes 98312 | tf_op jit(solution)/shard_map/ppermute | solution.py:20
  133.5 20.4 %collective-permute-start.4 = (bf16[1,1,128,128]{3,2,1,0:T(8,128)(2,1)S(1)}, bf16[1,1,128,128]{3,2,1,0:T(8,128)(2,1)S(1)}, u32[]{:S(2)}, u32[]{:S(2)}) collective-permute-start(bf16[1,1,128,128]{3,2,1,0:T(8,128)(2,1)S(1)} %fusion.48), channel_id=1, source_target_pairs={{0,8},{8,16},{16,24},{24,32},{32,40},{40,48},{48,56},{56,64},{64,7... | collective-permute-start | bytes 98312 | tf_op jit(solution)/shard_map/ppermute | solution.py:18
  153.9 16.5 %collective-permute-start.6 = (bf16[3,1,128,128]{3,2,1,0:T(8,128)(2,1)S(1)}, bf16[3,1,128,128]{3,2,1,0:T(8,128)(2,1)S(1)}, u32[]{:S(2)}, u32[]{:S(2)}) collective-permute-start(bf16[3,1,128,128]{3,2,1,0:T(8,128)(2,1)S(1)} %pad_maximum_fusion.2), channel_id=1, source_target_pairs={{0,1},{1,2},{2,3},{3,4},{4,5},{5,6},{6,7},{8,9},{9,10},{10,11},{11... | collective-permute-start | bytes 294920 | tf_op jit(solution)/shard_map/ppermute | solution.py:18
  155.9 20.2 %collective-permute-start.7 = (bf16[3,1,128,128]{3,2,1,0:T(8,128)(2,1)S(1)}, bf16[3,1,128,128]{3,2,1,0:T(8,128)(2,1)S(1)}, u32[]{:S(2)}, u32[]{:S(2)}) collective-permute-start(bf16[3,1,128,128]{3,2,1,0:T(8,128)(2,1)S(1)} %pad_maximum_fusion.2), channel_id=1, source_target_pairs={{1,0},{2,1},{3,2},{4,3},{5,4},{6,5},{7,6},{9,8},{10,9},{11,10},{12... | collective-permute-start | bytes 294920 | tf_op jit(solution)/shard_map/ppermute | solution.py:20
